TPU v7x, 512 devices: a whole 4x8x8 slice. The times are simulated.
512 devices in a mesh: dp: 128 (over y, z, core), mp: 4 (over x).
Axes of the slice: x: 4, y: 8, z: 8, core: 2. Of those that a mesh axis runs over, the one named last changes fastest.
Arguments:
- query_hidden: bfloat16 [4096, 32, 768], P('dp', None, 'mp'), may hold values from -6 to 6
- query_proj: bfloat16 [768, 128], P('mp'), may hold values from -0.21875 to 0.21875
- passages: bfloat16 [8192, 128, 128], P(('dp', 'mp')), may hold values from -6 to 6
- teacher: float32 [4096, 4, 64], P('dp'), may hold values from -8 to 8
- neg_blocks: int32 [4096, 4], P('dp'), may hold values from 0 to 127, all different within a row; in each aligned block of 32 rows (0 to 31, 32 to 63, ...) at most 2 rows name the same one
Outputs:
- kl_loss: float32 [4096], P('dp')
Inputs may be any that keep to these rules, and one draw needn't show every extreme that they name: `neg_blocks`: each query names 4 different blocks. Among the 32 queries of one dp index no block is named more than 2 times, and some block is named exactly 2 times.
All inputs are finite; a program needn't handle non-finite values.
Results may differ from a plain program's by a relative error of at most 0.0003.
Values may be sent and summed in bfloat16 or wider, within the bound.
No kernel may reach another device: no remote copies, remote signals or barrier semaphores. Data moves between devices by JAX's collectives and lax.ppermute only.
A program may use at most 64 MiB of HBM per device.

v0:
```python
import jax
import jax.numpy as jnp
from jax import lax
from jax.sharding import PartitionSpec as P

softness = 0.1


def unit_rows(values):
    return values * lax.rsqrt(jnp.sum(values * values, axis=-1, keepdims=True) + 1e-06)


def soft_scores(slot_rows, passage_vecs):
    slot_count = slot_rows.shape[0]
    block_size = 16
    padded_count = -(-slot_count // block_size) * block_size
    blocked = slot_rows.reshape(
        padded_count // block_size, block_size, slot_rows.shape[1], slot_rows.shape[2]
    )

    def block_scores(slot_block):
        sims = jnp.einsum(
            "sie,pje->sipj", slot_block, passage_vecs, preferred_element_type=jnp.float32
        )
        softened = softness * jnp.log(jnp.sum(jnp.exp(sims / softness), axis=-1))
        return jnp.sum(softened, axis=1)

    scored = lax.map(block_scores, blocked)
    return scored.reshape(padded_count, -1)


def per_device(query_hidden, query_proj, passages, teacher, neg_blocks):
    partial_sum = jnp.einsum(
        "qth,he->qte", query_hidden, query_proj, preferred_element_type=jnp.float32
    )
    passage_vecs = unit_rows(passages.astype(jnp.float32)).astype(jnp.bfloat16)
    dp_count = lax.axis_size("dp")
    query_count, pick_count = neg_blocks.shape
    embed_width = partial_sum.shape[2]
    row_count = query_count * pick_count
    capacity = max(2, -(-row_count // dp_count))
    slots_all = dp_count * capacity
    owners = neg_blocks.reshape(row_count)
    owner_hits = (owners[:, None] == jnp.arange(dp_count, dtype=jnp.int32)[None, :]).astype(
        jnp.int32
    )
    earlier = jnp.cumsum(owner_hits, axis=0) - owner_hits
    slot_rank = jnp.sum(earlier * owner_hits, axis=1)
    slot_ids = owners * capacity + slot_rank
    matches = (slot_ids[None, :] == jnp.arange(slots_all, dtype=jnp.int32)[:, None]).astype(
        jnp.int32
    )
    row_query = jnp.arange(row_count, dtype=jnp.int32) // pick_count
    source = jnp.sum(matches * row_query[None, :], axis=1)
    filled = jnp.sum(matches, axis=1)
    projected = lax.psum(partial_sum, "mp")
    query_vecs = unit_rows(projected).astype(jnp.bfloat16)
    tokens = query_vecs.shape[1]
    outgoing = query_vecs[source] * filled[:, None, None].astype(jnp.bfloat16)
    outgoing = outgoing.reshape(dp_count, capacity, tokens, embed_width)
    arrived_items = lax.all_to_all(outgoing, "dp", split_axis=0, concat_axis=0, tiled=True)
    dims_items = arrived_items.shape
    flat_items = arrived_items.reshape(dims_items[0] * dims_items[1], dims_items[2], dims_items[3])
    scores = soft_scores(flat_items, passage_vecs).reshape(dims_items[0], dims_items[1], -1)
    returned = lax.all_to_all(scores, "dp", split_axis=0, concat_axis=0, tiled=True)
    home_scores = returned.reshape(slots_all, -1)[slot_ids].reshape(query_count, pick_count, -1)
    teacher_logp = teacher - jnp.log(jnp.sum(jnp.exp(teacher), axis=(1, 2), keepdims=True))
    student = lax.all_gather(home_scores, "mp", axis=2, tiled=True)
    kl_loss = jnp.sum(jnp.exp(teacher_logp) * (teacher_logp - student), axis=(1, 2)) + jnp.log(
        jnp.sum(jnp.exp(student), axis=(1, 2))
    )
    return kl_loss


def solution(mesh):
    in_specs = (
        P("dp", None, "mp"),
        P("mp", None),
        P(("dp", "mp"), None, None),
        P("dp", None, None),
        P("dp", None),
    )
    out_specs = P("dp")
    return jax.shard_map(
        per_device, mesh=mesh, in_specs=in_specs, out_specs=out_specs, check_vma=False
    )
```

profile of v0, /device:TPU:8, one launch (start us, length us, event | category | flops | bytes accessed | tf_op | source)
XLA Modules:
  0.0 229.7 jit_solution(16609151651576874862)
XLA Ops:
  6.5 1.0 copy-done
  7.6 1.9 fusion.7
  9.5 0.8 copy.19
  11.2 57.0 %all-reduce.2.cloned.1.call-done = f32[32,32,128]{2,1,0:T(8,128)} async-done(((f32[32,32,128]{2,1,0:T(8,128)}), f32[32,32,128]{2,1,0:T(8,128)}) %all-reduce.2.cloned.1.call-update) | async-done | bytes 524304 | tf_op jit(solution)/shard_map/psum | solution.py:56
  68.2 1.2 multiply_reduce_fusion.1
  69.4 1.2 multiply_convert_fusion
  70.7 1.0 gather_fusion
  71.7 1.7 broadcast_multiply_fusion
  73.4 14.3 %all-to-all-start = ((bf16[128,2,32,128]{3,2,1,0:T(8,128)(2,1)}), bf16[128,2,32,128]{3,2,1,0:T(8,128)(2,1)S(1)}, u32[]{:S(2)}, u32[]{:S(2)}) async-start(bf16[128,2,32,128]{3,2,1,0:T(8,128)(2,1)} %broadcast_multiply_fusion), calls=%async_computation | async-start | bytes 4194304 | tf_op jit(solution)/shard_map/all_to_all | solution.py:61
  88.6 1.1 fusion.5
  89.8 50.3 %all-to-all-done = bf16[128,2,32,128]{3,2,1,0:T(8,128)(2,1)S(1)} async-done(((bf16[128,2,32,128]{3,2,1,0:T(8,128)(2,1)}), bf16[128,2,32,128]{3,2,1,0:T(8,128)(2,1)S(1)}, u32[]{:S(2)}, u32[]{:S(2)}) %all-to-all-start) | async-done | bytes 2097184 | tf_op jit(solution)/shard_map/all_to_all | solution.py:61
  140.1 49.7 %while.10 = (s32[]{:T(128)}, f32[16,16,16]{2,1,0:T(8,128)}, bf16[16,16,32,128]{3,2,1,0:T(8,128)(2,1)S(1)}, bf16[16,128,128]{2,1,0:T(8,128)(2,1)}, s32[]{:T(128)}) while((s32[]{:T(128)}, f32[16,16,16]{2,1,0:T(8,128)}, bf16[16,16,32,128]{3,2,1,0:T(8,128)(2,1)S(1)}, bf16[16,128,128]{2,1,0:T(8,128)(2,1)}, s32[]{:T(128)}) %tuple.25), condition=%wide.region_11.12_spmd, body=%wide.region_8.11_spmd.sunk | while | flops 270540544 | bytes 731713 | solution.py:28
  140.1 2.4 %exponential_reduce_fusion.4 = f32[16,32,16]{1,2,0:T(8,128)S(1)} fusion(bf16[16,128,128]{2,1,0:T(8,128)(2,1)} %get-tuple-element.78, bf16[16,16,32,128]{3,2,1,0:T(8,128)(2,1)S(1)} %get-tuple-element.77, s32[]{:T(128)} %get-tuple-element.70), kind=kOutput, calls=%fused_computation.2.clone.1 | convolution fusion | flops 270524416 | bytes 688132 | tf_op jit(solution)/shard_map/while/body/eval_jaxpr/sie,pje->sipj/dot_general | solution.py:22
  143.2 2.4 %exponential_reduce_fusion.4 = f32[16,32,16]{1,2,0:T(8,128)S(1)} fusion(bf16[16,128,128]{2,1,0:T(8,128)(2,1)} %get-tuple-element.78, bf16[16,16,32,128]{3,2,1,0:T(8,128)(2,1)S(1)} %get-tuple-element.77, s32[]{:T(128)} %get-tuple-element.70), kind=kOutput, calls=%fused_computation.2.clone.1 | convolution fusion | flops 270524416 | bytes 688132 | tf_op jit(solution)/shard_map/while/body/eval_jaxpr/sie,pje->sipj/dot_general | solution.py:22
  146.3 2.4 %exponential_reduce_fusion.4 = f32[16,32,16]{1,2,0:T(8,128)S(1)} fusion(bf16[16,128,128]{2,1,0:T(8,128)(2,1)} %get-tuple-element.78, bf16[16,16,32,128]{3,2,1,0:T(8,128)(2,1)S(1)} %get-tuple-element.77, s32[]{:T(128)} %get-tuple-element.70), kind=kOutput, calls=%fused_computation.2.clone.1 | convolution fusion | flops 270524416 | bytes 688132 | tf_op jit(solution)/shard_map/while/body/eval_jaxpr/sie,pje->sipj/dot_general | solution.py:22
  149.4 2.4 %exponential_reduce_fusion.4 = f32[16,32,16]{1,2,0:T(8,128)S(1)} fusion(bf16[16,128,128]{2,1,0:T(8,128)(2,1)} %get-tuple-element.78, bf16[16,16,32,128]{3,2,1,0:T(8,128)(2,1)S(1)} %get-tuple-element.77, s32[]{:T(128)} %get-tuple-element.70), kind=kOutput, calls=%fused_computation.2.clone.1 | convolution fusion | flops 270524416 | bytes 688132 | tf_op jit(solution)/shard_map/while/body/eval_jaxpr/sie,pje->sipj/dot_general | solution.py:22
  152.5 2.4 %exponential_reduce_fusion.4 = f32[16,32,16]{1,2,0:T(8,128)S(1)} fusion(bf16[16,128,128]{2,1,0:T(8,128)(2,1)} %get-tuple-element.78, bf16[16,16,32,128]{3,2,1,0:T(8,128)(2,1)S(1)} %get-tuple-element.77, s32[]{:T(128)} %get-tuple-element.70), kind=kOutput, calls=%fused_computation.2.clone.1 | convolution fusion | flops 270524416 | bytes 688132 | tf_op jit(solution)/shard_map/while/body/eval_jaxpr/sie,pje->sipj/dot_general | solution.py:22
  155.6 2.4 %exponential_reduce_fusion.4 = f32[16,32,16]{1,2,0:T(8,128)S(1)} fusion(bf16[16,128,128]{2,1,0:T(8,128)(2,1)} %get-tuple-element.78, bf16[16,16,32,128]{3,2,1,0:T(8,128)(2,1)S(1)} %get-tuple-element.77, s32[]{:T(128)} %get-tuple-element.70), kind=kOutput, calls=%fused_computation.2.clone.1 | convolution fusion | flops 270524416 | bytes 688132 | tf_op jit(solution)/shard_map/while/body/eval_jaxpr/sie,pje->sipj/dot_general | solution.py:22
  158.7 2.4 %exponential_reduce_fusion.4 = f32[16,32,16]{1,2,0:T(8,128)S(1)} fusion(bf16[16,128,128]{2,1,0:T(8,128)(2,1)} %get-tuple-element.78, bf16[16,16,32,128]{3,2,1,0:T(8,128)(2,1)S(1)} %get-tuple-element.77, s32[]{:T(128)} %get-tuple-element.70), kind=kOutput, calls=%fused_computation.2.clone.1 | convolution fusion | flops 270524416 | bytes 688132 | tf_op jit(solution)/shard_map/while/body/eval_jaxpr/sie,pje->sipj/dot_general | solution.py:22
  161.8 2.4 %exponential_reduce_fusion.4 = f32[16,32,16]{1,2,0:T(8,128)S(1)} fusion(bf16[16,128,128]{2,1,0:T(8,128)(2,1)} %get-tuple-element.78, bf16[16,16,32,128]{3,2,1,0:T(8,128)(2,1)S(1)} %get-tuple-element.77, s32[]{:T(128)} %get-tuple-element.70), kind=kOutput, calls=%fused_computation.2.clone.1 | convolution fusion | flops 270524416 | bytes 688132 | tf_op jit(solution)/shard_map/while/body/eval_jaxpr/sie,pje->sipj/dot_general | solution.py:22
  164.9 2.4 %exponential_reduce_fusion.4 = f32[16,32,16]{1,2,0:T(8,128)S(1)} fusion(bf16[16,128,128]{2,1,0:T(8,128)(2,1)} %get-tuple-element.78, bf16[16,16,32,128]{3,2,1,0:T(8,128)(2,1)S(1)} %get-tuple-element.77, s32[]{:T(128)} %get-tuple-element.70), kind=kOutput, calls=%fused_computation.2.clone.1 | convolution fusion | flops 270524416 | bytes 688132 | tf_op jit(solution)/shard_map/while/body/eval_jaxpr/sie,pje->sipj/dot_general | solution.py:22
  168.0 2.4 %exponential_reduce_fusion.4 = f32[16,32,16]{1,2,0:T(8,128)S(1)} fusion(bf16[16,128,128]{2,1,0:T(8,128)(2,1)} %get-tuple-element.78, bf16[16,16,32,128]{3,2,1,0:T(8,128)(2,1)S(1)} %get-tuple-element.77, s32[]{:T(128)} %get-tuple-element.70), kind=kOutput, calls=%fused_computation.2.clone.1 | convolution fusion | flops 270524416 | bytes 688132 | tf_op jit(solution)/shard_map/while/body/eval_jaxpr/sie,pje->sipj/dot_general | solution.py:22
  171.1 2.4 %exponential_reduce_fusion.4 = f32[16,32,16]{1,2,0:T(8,128)S(1)} fusion(bf16[16,128,128]{2,1,0:T(8,128)(2,1)} %get-tuple-element.78, bf16[16,16,32,128]{3,2,1,0:T(8,128)(2,1)S(1)} %get-tuple-element.77, s32[]{:T(128)} %get-tuple-element.70), kind=kOutput, calls=%fused_computation.2.clone.1 | convolution fusion | flops 270524416 | bytes 688132 | tf_op jit(solution)/shard_map/while/body/eval_jaxpr/sie,pje->sipj/dot_general | solution.py:22
  174.2 2.4 %exponential_reduce_fusion.4 = f32[16,32,16]{1,2,0:T(8,128)S(1)} fusion(bf16[16,128,128]{2,1,0:T(8,128)(2,1)} %get-tuple-element.78, bf16[16,16,32,128]{3,2,1,0:T(8,128)(2,1)S(1)} %get-tuple-element.77, s32[]{:T(128)} %get-tuple-element.70), kind=kOutput, calls=%fused_computation.2.clone.1 | convolution fusion | flops 270524416 | bytes 688132 | tf_op jit(solution)/shard_map/while/body/eval_jaxpr/sie,pje->sipj/dot_general | solution.py:22
  177.4 2.4 %exponential_reduce_fusion.4 = f32[16,32,16]{1,2,0:T(8,128)S(1)} fusion(bf16[16,128,128]{2,1,0:T(8,128)(2,1)} %get-tuple-element.78, bf16[16,16,32,128]{3,2,1,0:T(8,128)(2,1)S(1)} %get-tuple-element.77, s32[]{:T(128)} %get-tuple-element.70), kind=kOutput, calls=%fused_computation.2.clone.1 | convolution fusion | flops 270524416 | bytes 688132 | tf_op jit(solution)/shard_map/while/body/eval_jaxpr/sie,pje->sipj/dot_general | solution.py:22
  180.5 2.4 %exponential_reduce_fusion.4 = f32[16,32,16]{1,2,0:T(8,128)S(1)} fusion(bf16[16,128,128]{2,1,0:T(8,128)(2,1)} %get-tuple-element.78, bf16[16,16,32,128]{3,2,1,0:T(8,128)(2,1)S(1)} %get-tuple-element.77, s32[]{:T(128)} %get-tuple-element.70), kind=kOutput, calls=%fused_computation.2.clone.1 | convolution fusion | flops 270524416 | bytes 688132 | tf_op jit(solution)/shard_map/while/body/eval_jaxpr/sie,pje->sipj/dot_general | solution.py:22
  183.6 2.4 %exponential_reduce_fusion.4 = f32[16,32,16]{1,2,0:T(8,128)S(1)} fusion(bf16[16,128,128]{2,1,0:T(8,128)(2,1)} %get-tuple-element.78, bf16[16,16,32,128]{3,2,1,0:T(8,128)(2,1)S(1)} %get-tuple-element.77, s32[]{:T(128)} %get-tuple-element.70), kind=kOutput, calls=%fused_computation.2.clone.1 | convolution fusion | flops 270524416 | bytes 688132 | tf_op jit(solution)/shard_map/while/body/eval_jaxpr/sie,pje->sipj/dot_general | solution.py:22
  186.7 2.4 %exponential_reduce_fusion.4 = f32[16,32,16]{1,2,0:T(8,128)S(1)} fusion(bf16[16,128,128]{2,1,0:T(8,128)(2,1)} %get-tuple-element.78, bf16[16,16,32,128]{3,2,1,0:T(8,128)(2,1)S(1)} %get-tuple-element.77, s32[]{:T(128)} %get-tuple-element.70), kind=kOutput, calls=%fused_computation.2.clone.1 | convolution fusion | flops 270524416 | bytes 688132 | tf_op jit(solution)/shard_map/while/body/eval_jaxpr/sie,pje->sipj/dot_general | solution.py:22
  189.8 7.5 %all-to-all-start.1 = ((f32[128,2,16]{2,1,0:T(2,128)}), f32[128,2,16]{2,1,0:T(2,128)S(1)}, u32[]{:S(2)}, u32[]{:S(2)}) async-start(f32[128,2,16]{2,1,0:T(2,128)} %bitcast.10), calls=%async_computation.1 | async-start | bytes 262144 | tf_op jit(solution)/shard_map/all_to_all | solution.py:65
  197.3 11.9 %all-to-all-done.1 = f32[128,2,16]{2,1,0:T(2,128)S(1)} async-done(((f32[128,2,16]{2,1,0:T(2,128)}), f32[128,2,16]{2,1,0:T(2,128)S(1)}, u32[]{:S(2)}, u32[]{:S(2)}) %all-to-all-start.1) | async-done | bytes 16416 | tf_op jit(solution)/shard_map/all_to_all | solution.py:65
  209.2 0.6 gather_fusion.1
  209.9 12.0 %all_gather.3 = f32[32,4,64]{0,1,2:T(4,128)S(1)} all-gather(f32[32,4,16]{0,1,2:T(4,128)S(1)} %copy.21), channel_id=1, replica_groups=mesh['dp'=128,'mp'=4] {'mp'}, dimensions={2}, use_global_device_ids=true | all-gather | bytes 40960 | tf_op jit(solution)/shard_map/all_gather | solution.py:68
  (67 shorter events, 14.3 us)
Async XLA Ops:
  6.5 1.0 copy-start
  6.5 61.6 %all-reduce.2.cloned.1.call-start = ((), (), s32[]{:S(2)}) async-start(), calls=%async_computation.2 | async-start | bytes 1048576 | tf_op jit(solution)/shard_map/psum | solution.py:56
  73.4 14.3 %copy-start.3 = (s32[32,4]{0,1:T(4,128)S(1)}, s32[32,4]{0,1:T(4,128)}, u32[]{:S(2)}) copy-start(s32[32,4]{0,1:T(4,128)} %param.11) | copy-start | bytes 1540
  73.4 14.5 %copy-start.2 = (f32[32,4,64]{2,1,0:T(4,128)S(1)}, f32[32,4,64]{2,1,0:T(4,128)}, u32[]{:S(2)}) copy-start(f32[32,4,64]{2,1,0:T(4,128)} %param.10) | copy-start | bytes 98308
  73.4 14.9 %copy-start.1 = (bf16[16,128,128]{2,1,0:T(8,128)(2,1)S(1)}, bf16[16,128,128]{2,1,0:T(8,128)(2,1)}, u32[]{:S(2)}) copy-start(bf16[16,128,128]{2,1,0:T(8,128)(2,1)} %param.9) | copy-start | bytes 1572868
  73.4 66.7 %all-to-all-start = ((bf16[128,2,32,128]{3,2,1,0:T(8,128)(2,1)}), bf16[128,2,32,128]{3,2,1,0:T(8,128)(2,1)S(1)}, u32[]{:S(2)}, u32[]{:S(2)}) async-start(bf16[128,2,32,128]{3,2,1,0:T(8,128)(2,1)} %broadcast_multiply_fusion), calls=%async_computation | async-start | bytes 4194304 | tf_op jit(solution)/shard_map/all_to_all | solution.py:61
  189.8 19.4 %all-to-all-start.1 = ((f32[128,2,16]{2,1,0:T(2,128)}), f32[128,2,16]{2,1,0:T(2,128)S(1)}, u32[]{:S(2)}, u32[]{:S(2)}) async-start(f32[128,2,16]{2,1,0:T(2,128)} %bitcast.10), calls=%async_computation.1 | async-start | bytes 262144 | tf_op jit(solution)/shard_map/all_to_all | solution.py:65
Sparse Core Ops, SparseCore 0:
  9.7 58.4 all-reduce.1
where the time goes:
time: 231 us; the launch traced here: 230 us
  waiting for transfers between devices  119 us (52%)
  matrix products  39.9 us (17%)
  starting transfers between devices  21.8 us (9%)
  local copies, waits for them, and re-layouts  13.7 us (6%)
  between operations  13.6 us (6%)
  blocking collectives  12 us (5%)
  other arithmetic  9.3 us (4%)
    psum x1, waiting for transfers between devices, per_device(): projected = lax.psum(partial_sum, 'mp')  57 us
    all_to_all x1, waiting for transfers between devices, per_device(): lax.all_to_all(outgoing, 'dp', split_axis=0, concat_axis=0, tiled=True)  50.3 us
    dot_general x16, matrix products, block_scores(): jnp.einsum('sie,pje->sipj', slot_block, passage_vecs, preferred_element_t...  38 us
    all_to_all x1, starting transfers between devices, per_device(): lax.all_to_all(outgoing, 'dp', split_axis=0, concat_axis=0, tiled=True)  14.3 us
    all_gather x1, blocking collectives, per_device(): student = lax.all_gather(home_scores, 'mp', axis=2, tiled=True)  12 us
    all_to_all x1, waiting for transfers between devices, per_device(): lax.all_to_all(scores, 'dp', split_axis=0, concat_axis=0, tiled=True)  11.9 us
    dynamic_update_slice x16, local copies, waits for them, and re-layouts, soft_scores(): scored = lax.map(block_scores, blocked)  9.63 us
    all_to_all x1, starting transfers between devices, per_device(): lax.all_to_all(scores, 'dp', split_axis=0, concat_axis=0, tiled=True)  7.48 us
  transfers between devices with their start and end apart: 3, of which 3 were waited for; matrix products, arithmetic and copies ran while one was open for 2% of the time, Pallas kernels for 0%

commit v1 on v0

--- a/solution.py
+++ b/solution.py
@@ -53,7 +53,17 @@
     row_query = jnp.arange(row_count, dtype=jnp.int32) // pick_count
     source = jnp.sum(matches * row_query[None, :], axis=1)
     filled = jnp.sum(matches, axis=1)
-    projected = lax.psum(partial_sum, "mp")
+
+    def lay_seats_all_by_axis(arr):
+        near = arr
+        n_axis = lax.axis_size("mp")
+        for jj in [
+            [(t, t ^ dev_j) for t in range(n_axis)] for dev_j in (1, 2, 4, 8, 16) if dev_j < n_axis
+        ]:
+            near = near + lax.ppermute(near, "mp", jj)
+        return near
+
+    projected = lay_seats_all_by_axis(partial_sum)
     query_vecs = unit_rows(projected).astype(jnp.bfloat16)
     tokens = query_vecs.shape[1]
     outgoing = query_vecs[source] * filled[:, None, None].astype(jnp.bfloat16)

time: 231 us -> 192 us (0.83)
  the two profiles are of different devices: /device:TPU:8 before, /device:TPU:2 now
where the time goes in v1:
time: 192 us; the launch traced here: 191 us
  waiting for transfers between devices  79.7 us (42%)
  matrix products  39.1 us (20%)
  starting transfers between devices  38.4 us (20%)
  local copies, waits for them, and re-layouts  13.7 us (7%)
  blocking collectives  12 us (6%)
  other arithmetic  7.3 us (4%)
    all_to_all x1, waiting for transfers between devices, per_device(): lax.all_to_all(outgoing, 'dp', split_axis=0, concat_axis=0, tiled=True)  50.3 us
    dot_general x16, matrix products, block_scores(): jnp.einsum('sie,pje->sipj', slot_block, passage_vecs, preferred_element_t...  38 us
    all_to_all x1, starting transfers between devices, per_device(): lax.all_to_all(outgoing, 'dp', split_axis=0, concat_axis=0, tiled=True)  19.1 us
    ppermute x2, waiting for transfers between devices, lay_seats_all_by_axis(): near = near + lax.ppermute(near, 'mp', jj)  17.1 us
    all_to_all x1, waiting for transfers between devices, per_device(): lax.all_to_all(scores, 'dp', split_axis=0, concat_axis=0, tiled=True)  12.3 us
    all_gather x1, blocking collectives, per_device(): student = lax.all_gather(home_scores, 'mp', axis=2, tiled=True)  12 us
    ppermute x2, starting transfers between devices, lay_seats_all_by_axis(): near = near + lax.ppermute(near, 'mp', jj)  11.8 us
    dynamic_update_slice x16, local copies, waits for them, and re-layouts, soft_scores(): scored = lax.map(block_scores, blocked)  9.63 us
  transfers between devices with their start and end apart: 4, of which 4 were waited for; matrix products, arithmetic and copies ran while one was open for 2% of the time, Pallas kernels for 0%

profile of v1, /device:TPU:2, one launch (start us, length us, event | category | flops | bytes accessed | tf_op | source)
XLA Modules:
  0.0 190.6 jit_solution(9149132172182549748)
XLA Ops:
  0.0 1.0 copy-done
  1.0 1.1 fusion.7
  2.1 7.8 %collective-permute-start = (f32[32,32,128]{2,1,0:T(8,128)S(1)}, f32[32,32,128]{2,1,0:T(8,128)S(1)}, u32[]{:S(2)}, u32[]{:S(2)}) collective-permute-start(f32[32,32,128]{2,1,0:T(8,128)S(1)} %fusion.7), channel_id=1, source_target_pairs={{0,1},{1,0},{2,3},{3,2},{4,5},{5,4},{6,7},{7,6},{8,9},{9,8},{10,11... | collective-permute-start | bytes 1572872 | tf_op jit(solution)/shard_map/ppermute | solution.py:63
  9.9 0.8 copy.19
  11.2 6.5 %collective-permute-done = f32[32,32,128]{2,1,0:T(8,128)S(1)} collective-permute-done((f32[32,32,128]{2,1,0:T(8,128)S(1)}, f32[32,32,128]{2,1,0:T(8,128)S(1)}, u32[]{:S(2)}, u32[]{:S(2)}) %collective-permute-start) | collective-permute-done | bytes 524320 | tf_op jit(solution)/shard_map/ppermute | solution.py:63
  17.8 4.0 %collective-permute-start.1 = (f32[32,32,128]{2,1,0:T(8,128)S(1)}, f32[32,32,128]{2,1,0:T(8,128)S(1)}, u32[]{:S(2)}, u32[]{:S(2)}) collective-permute-start(f32[32,32,128]{2,1,0:T(8,128)S(1)} %add.81), channel_id=1, source_target_pairs={{0,2},{1,3},{2,0},{3,1},{4,6},{5,7},{6,4},{7,5},{8,10},{9,11},{10,... | collective-permute-start | bytes 1572872 | tf_op jit(solution)/shard_map/ppermute | solution.py:63
  22.2 10.7 %collective-permute-done.1 = f32[32,32,128]{2,1,0:T(8,128)S(1)} collective-permute-done((f32[32,32,128]{2,1,0:T(8,128)S(1)}, f32[32,32,128]{2,1,0:T(8,128)S(1)}, u32[]{:S(2)}, u32[]{:S(2)}) %collective-permute-start.1) | collective-permute-done | bytes 524320 | tf_op jit(solution)/shard_map/ppermute | solution.py:63
  33.3 1.0 gather_fusion
  34.3 1.7 broadcast_multiply_fusion
  36.0 19.1 %all-to-all-start = ((bf16[128,2,32,128]{3,2,1,0:T(8,128)(2,1)}), bf16[128,2,32,128]{3,2,1,0:T(8,128)(2,1)S(1)}, u32[]{:S(2)}, u32[]{:S(2)}) async-start(bf16[128,2,32,128]{3,2,1,0:T(8,128)(2,1)} %broadcast_multiply_fusion), calls=%async_computation | async-start | bytes 4194304 | tf_op jit(solution)/shard_map/all_to_all | solution.py:71
  56.0 1.1 fusion.5
  57.1 50.3 %all-to-all-done = bf16[128,2,32,128]{3,2,1,0:T(8,128)(2,1)S(1)} async-done(((bf16[128,2,32,128]{3,2,1,0:T(8,128)(2,1)}), bf16[128,2,32,128]{3,2,1,0:T(8,128)(2,1)S(1)}, u32[]{:S(2)}, u32[]{:S(2)}) %all-to-all-start) | async-done | bytes 2097184 | tf_op jit(solution)/shard_map/all_to_all | solution.py:71
  107.4 49.7 %while.10 = (s32[]{:T(128)}, f32[16,16,16]{2,1,0:T(8,128)}, bf16[16,16,32,128]{3,2,1,0:T(8,128)(2,1)S(1)}, bf16[16,128,128]{2,1,0:T(8,128)(2,1)}, s32[]{:T(128)}) while((s32[]{:T(128)}, f32[16,16,16]{2,1,0:T(8,128)}, bf16[16,16,32,128]{3,2,1,0:T(8,128)(2,1)S(1)}, bf16[16,128,128]{2,1,0:T(8,128)(2,1)}, s32[]{:T(128)}) %tuple.24), condition=%wide.region_10.11_spmd, body=%wide.region_7.10_spmd.sunk | while | flops 270540544 | bytes 731713 | solution.py:28
  107.4 2.4 %exponential_reduce_fusion.4 = f32[16,32,16]{1,2,0:T(8,128)S(1)} fusion(bf16[16,128,128]{2,1,0:T(8,128)(2,1)} %get-tuple-element.80, bf16[16,16,32,128]{3,2,1,0:T(8,128)(2,1)S(1)} %get-tuple-element.79, s32[]{:T(128)} %get-tuple-element.72), kind=kOutput, calls=%fused_computation.2.clone.1 | convolution fusion | flops 270524416 | bytes 688132 | tf_op jit(solution)/shard_map/while/body/eval_jaxpr/sie,pje->sipj/dot_general | solution.py:22
  110.5 2.4 %exponential_reduce_fusion.4 = f32[16,32,16]{1,2,0:T(8,128)S(1)} fusion(bf16[16,128,128]{2,1,0:T(8,128)(2,1)} %get-tuple-element.80, bf16[16,16,32,128]{3,2,1,0:T(8,128)(2,1)S(1)} %get-tuple-element.79, s32[]{:T(128)} %get-tuple-element.72), kind=kOutput, calls=%fused_computation.2.clone.1 | convolution fusion | flops 270524416 | bytes 688132 | tf_op jit(solution)/shard_map/while/body/eval_jaxpr/sie,pje->sipj/dot_general | solution.py:22
  113.6 2.4 %exponential_reduce_fusion.4 = f32[16,32,16]{1,2,0:T(8,128)S(1)} fusion(bf16[16,128,128]{2,1,0:T(8,128)(2,1)} %get-tuple-element.80, bf16[16,16,32,128]{3,2,1,0:T(8,128)(2,1)S(1)} %get-tuple-element.79, s32[]{:T(128)} %get-tuple-element.72), kind=kOutput, calls=%fused_computation.2.clone.1 | convolution fusion | flops 270524416 | bytes 688132 | tf_op jit(solution)/shard_map/while/body/eval_jaxpr/sie,pje->sipj/dot_general | solution.py:22
  116.7 2.4 %exponential_reduce_fusion.4 = f32[16,32,16]{1,2,0:T(8,128)S(1)} fusion(bf16[16,128,128]{2,1,0:T(8,128)(2,1)} %get-tuple-element.80, bf16[16,16,32,128]{3,2,1,0:T(8,128)(2,1)S(1)} %get-tuple-element.79, s32[]{:T(128)} %get-tuple-element.72), kind=kOutput, calls=%fused_computation.2.clone.1 | convolution fusion | flops 270524416 | bytes 688132 | tf_op jit(solution)/shard_map/while/body/eval_jaxpr/sie,pje->sipj/dot_general | solution.py:22
  119.8 2.4 %exponential_reduce_fusion.4 = f32[16,32,16]{1,2,0:T(8,128)S(1)} fusion(bf16[16,128,128]{2,1,0:T(8,128)(2,1)} %get-tuple-element.80, bf16[16,16,32,128]{3,2,1,0:T(8,128)(2,1)S(1)} %get-tuple-element.79, s32[]{:T(128)} %get-tuple-element.72), kind=kOutput, calls=%fused_computation.2.clone.1 | convolution fusion | flops 270524416 | bytes 688132 | tf_op jit(solution)/shard_map/while/body/eval_jaxpr/sie,pje->sipj/dot_general | solution.py:22
  122.9 2.4 %exponential_reduce_fusion.4 = f32[16,32,16]{1,2,0:T(8,128)S(1)} fusion(bf16[16,128,128]{2,1,0:T(8,128)(2,1)} %get-tuple-element.80, bf16[16,16,32,128]{3,2,1,0:T(8,128)(2,1)S(1)} %get-tuple-element.79, s32[]{:T(128)} %get-tuple-element.72), kind=kOutput, calls=%fused_computation.2.clone.1 | convolution fusion | flops 270524416 | bytes 688132 | tf_op jit(solution)/shard_map/while/body/eval_jaxpr/sie,pje->sipj/dot_general | solution.py:22
  126.0 2.4 %exponential_reduce_fusion.4 = f32[16,32,16]{1,2,0:T(8,128)S(1)} fusion(bf16[16,128,128]{2,1,0:T(8,128)(2,1)} %get-tuple-element.80, bf16[16,16,32,128]{3,2,1,0:T(8,128)(2,1)S(1)} %get-tuple-element.79, s32[]{:T(128)} %get-tuple-element.72), kind=kOutput, calls=%fused_computation.2.clone.1 | convolution fusion | flops 270524416 | bytes 688132 | tf_op jit(solution)/shard_map/while/body/eval_jaxpr/sie,pje->sipj/dot_general | solution.py:22
  129.2 2.4 %exponential_reduce_fusion.4 = f32[16,32,16]{1,2,0:T(8,128)S(1)} fusion(bf16[16,128,128]{2,1,0:T(8,128)(2,1)} %get-tuple-element.80, bf16[16,16,32,128]{3,2,1,0:T(8,128)(2,1)S(1)} %get-tuple-element.79, s32[]{:T(128)} %get-tuple-element.72), kind=kOutput, calls=%fused_computation.2.clone.1 | convolution fusion | flops 270524416 | bytes 688132 | tf_op jit(solution)/shard_map/while/body/eval_jaxpr/sie,pje->sipj/dot_general | solution.py:22
  132.3 2.4 %exponential_reduce_fusion.4 = f32[16,32,16]{1,2,0:T(8,128)S(1)} fusion(bf16[16,128,128]{2,1,0:T(8,128)(2,1)} %get-tuple-element.80, bf16[16,16,32,128]{3,2,1,0:T(8,128)(2,1)S(1)} %get-tuple-element.79, s32[]{:T(128)} %get-tuple-element.72), kind=kOutput, calls=%fused_computation.2.clone.1 | convolution fusion | flops 270524416 | bytes 688132 | tf_op jit(solution)/shard_map/while/body/eval_jaxpr/sie,pje->sipj/dot_general | solution.py:22
  135.4 2.4 %exponential_reduce_fusion.4 = f32[16,32,16]{1,2,0:T(8,128)S(1)} fusion(bf16[16,128,128]{2,1,0:T(8,128)(2,1)} %get-tuple-element.80, bf16[16,16,32,128]{3,2,1,0:T(8,128)(2,1)S(1)} %get-tuple-element.79, s32[]{:T(128)} %get-tuple-element.72), kind=kOutput, calls=%fused_computation.2.clone.1 | convolution fusion | flops 270524416 | bytes 688132 | tf_op jit(solution)/shard_map/while/body/eval_jaxpr/sie,pje->sipj/dot_general | solution.py:22
  138.5 2.4 %exponential_reduce_fusion.4 = f32[16,32,16]{1,2,0:T(8,128)S(1)} fusion(bf16[16,128,128]{2,1,0:T(8,128)(2,1)} %get-tuple-element.80, bf16[16,16,32,128]{3,2,1,0:T(8,128)(2,1)S(1)} %get-tuple-element.79, s32[]{:T(128)} %get-tuple-element.72), kind=kOutput, calls=%fused_computation.2.clone.1 | convolution fusion | flops 270524416 | bytes 688132 | tf_op jit(solution)/shard_map/while/body/eval_jaxpr/sie,pje->sipj/dot_general | solution.py:22
  141.6 2.4 %exponential_reduce_fusion.4 = f32[16,32,16]{1,2,0:T(8,128)S(1)} fusion(bf16[16,128,128]{2,1,0:T(8,128)(2,1)} %get-tuple-element.80, bf16[16,16,32,128]{3,2,1,0:T(8,128)(2,1)S(1)} %get-tuple-element.79, s32[]{:T(128)} %get-tuple-element.72), kind=kOutput, calls=%fused_computation.2.clone.1 | convolution fusion | flops 270524416 | bytes 688132 | tf_op jit(solution)/shard_map/while/body/eval_jaxpr/sie,pje->sipj/dot_general | solution.py:22
  144.7 2.4 %exponential_reduce_fusion.4 = f32[16,32,16]{1,2,0:T(8,128)S(1)} fusion(bf16[16,128,128]{2,1,0:T(8,128)(2,1)} %get-tuple-element.80, bf16[16,16,32,128]{3,2,1,0:T(8,128)(2,1)S(1)} %get-tuple-element.79, s32[]{:T(128)} %get-tuple-element.72), kind=kOutput, calls=%fused_computation.2.clone.1 | convolution fusion | flops 270524416 | bytes 688132 | tf_op jit(solution)/shard_map/while/body/eval_jaxpr/sie,pje->sipj/dot_general | solution.py:22
  147.8 2.4 %exponential_reduce_fusion.4 = f32[16,32,16]{1,2,0:T(8,128)S(1)} fusion(bf16[16,128,128]{2,1,0:T(8,128)(2,1)} %get-tuple-element.80, bf16[16,16,32,128]{3,2,1,0:T(8,128)(2,1)S(1)} %get-tuple-element.79, s32[]{:T(128)} %get-tuple-element.72), kind=kOutput, calls=%fused_computation.2.clone.1 | convolution fusion | flops 270524416 | bytes 688132 | tf_op jit(solution)/shard_map/while/body/eval_jaxpr/sie,pje->sipj/dot_general | solution.py:22
  150.9 2.4 %exponential_reduce_fusion.4 = f32[16,32,16]{1,2,0:T(8,128)S(1)} fusion(bf16[16,128,128]{2,1,0:T(8,128)(2,1)} %get-tuple-element.80, bf16[16,16,32,128]{3,2,1,0:T(8,128)(2,1)S(1)} %get-tuple-element.79, s32[]{:T(128)} %get-tuple-element.72), kind=kOutput, calls=%fused_computation.2.clone.1 | convolution fusion | flops 270524416 | bytes 688132 | tf_op jit(solution)/shard_map/while/body/eval_jaxpr/sie,pje->sipj/dot_general | solution.py:22
  154.0 2.4 %exponential_reduce_fusion.4 = f32[16,32,16]{1,2,0:T(8,128)S(1)} fusion(bf16[16,128,128]{2,1,0:T(8,128)(2,1)} %get-tuple-element.80, bf16[16,16,32,128]{3,2,1,0:T(8,128)(2,1)S(1)} %get-tuple-element.79, s32[]{:T(128)} %get-tuple-element.72), kind=kOutput, calls=%fused_computation.2.clone.1 | convolution fusion | flops 270524416 | bytes 688132 | tf_op jit(solution)/shard_map/while/body/eval_jaxpr/sie,pje->sipj/dot_general | solution.py:22
  157.1 7.5 %all-to-all-start.1 = ((f32[128,2,16]{2,1,0:T(2,128)}), f32[128,2,16]{2,1,0:T(2,128)S(1)}, u32[]{:S(2)}, u32[]{:S(2)}) async-start(f32[128,2,16]{2,1,0:T(2,128)} %bitcast.10), calls=%async_computation.1 | async-start | bytes 262144 | tf_op jit(solution)/shard_map/all_to_all | solution.py:75
  164.7 12.3 %all-to-all-done.1 = f32[128,2,16]{2,1,0:T(2,128)S(1)} async-done(((f32[128,2,16]{2,1,0:T(2,128)}), f32[128,2,16]{2,1,0:T(2,128)S(1)}, u32[]{:S(2)}, u32[]{:S(2)}) %all-to-all-start.1) | async-done | bytes 16416 | tf_op jit(solution)/shard_map/all_to_all | solution.py:75
  177.7 12.0 %all_gather.3 = f32[32,4,64]{0,1,2:T(4,128)S(1)} all-gather(f32[32,4,16]{0,1,2:T(4,128)S(1)} %copy.21), channel_id=1, replica_groups=mesh['dp'=128,'mp'=4] {'mp'}, dimensions={2}, use_global_device_ids=true | all-gather | bytes 40960 | tf_op jit(solution)/shard_map/all_gather | solution.py:78
  (69 shorter events, 15.4 us)
Async XLA Ops:
  0.0 1.0 copy-start
  2.1 15.6 %collective-permute-start = (f32[32,32,128]{2,1,0:T(8,128)S(1)}, f32[32,32,128]{2,1,0:T(8,128)S(1)}, u32[]{:S(2)}, u32[]{:S(2)}) collective-permute-start(f32[32,32,128]{2,1,0:T(8,128)S(1)} %fusion.7), channel_id=1, source_target_pairs={{0,1},{1,0},{2,3},{3,2},{4,5},{5,4},{6,7},{7,6},{8,9},{9,8},{10,11... | collective-permute-start | bytes 1572872 | tf_op jit(solution)/shard_map/ppermute | solution.py:63
  17.8 15.1 %collective-permute-start.1 = (f32[32,32,128]{2,1,0:T(8,128)S(1)}, f32[32,32,128]{2,1,0:T(8,128)S(1)}, u32[]{:S(2)}, u32[]{:S(2)}) collective-permute-start(f32[32,32,128]{2,1,0:T(8,128)S(1)} %add.81), channel_id=1, source_target_pairs={{0,2},{1,3},{2,0},{3,1},{4,6},{5,7},{6,4},{7,5},{8,10},{9,11},{10,... | collective-permute-start | bytes 1572872 | tf_op jit(solution)/shard_map/ppermute | solution.py:63
  36.0 19.1 %copy-start.3 = (s32[32,4]{0,1:T(4,128)S(1)}, s32[32,4]{0,1:T(4,128)}, u32[]{:S(2)}) copy-start(s32[32,4]{0,1:T(4,128)} %param.11) | copy-start | bytes 1540
  36.0 19.3 %copy-start.2 = (f32[32,4,64]{2,1,0:T(4,128)S(1)}, f32[32,4,64]{2,1,0:T(4,128)}, u32[]{:S(2)}) copy-start(f32[32,4,64]{2,1,0:T(4,128)} %param.10) | copy-start | bytes 98308
  36.0 19.6 %copy-start.1 = (bf16[16,128,128]{2,1,0:T(8,128)(2,1)S(1)}, bf16[16,128,128]{2,1,0:T(8,128)(2,1)}, u32[]{:S(2)}) copy-start(bf16[16,128,128]{2,1,0:T(8,128)(2,1)} %param.9) | copy-start | bytes 1572868
  36.0 71.4 %all-to-all-start = ((bf16[128,2,32,128]{3,2,1,0:T(8,128)(2,1)}), bf16[128,2,32,128]{3,2,1,0:T(8,128)(2,1)S(1)}, u32[]{:S(2)}, u32[]{:S(2)}) async-start(bf16[128,2,32,128]{3,2,1,0:T(8,128)(2,1)} %broadcast_multiply_fusion), calls=%async_computation | async-start | bytes 4194304 | tf_op jit(solution)/shard_map/all_to_all | solution.py:71
  157.1 19.8 %all-to-all-start.1 = ((f32[128,2,16]{2,1,0:T(2,128)}), f32[128,2,16]{2,1,0:T(2,128)S(1)}, u32[]{:S(2)}, u32[]{:S(2)}) async-start(f32[128,2,16]{2,1,0:T(2,128)} %bitcast.10), calls=%async_computation.1 | async-start | bytes 262144 | tf_op jit(solution)/shard_map/all_to_all | solution.py:75
